TPU v7x, 256 devices: a whole 4x4x8 slice. The times are simulated.
256 devices in a mesh: group: 16 (over y, x), member: 16 (over z, core).
Axes of the slice: x: 4, y: 4, z: 8, core: 2. Of those that a mesh axis runs over, the one named last changes fastest.
Arguments:
- queries: bfloat16 [65536, 6144], P(('group', 'member')), may hold values from -64 to 64
- keys_values: bfloat16 [512, 128, 2048], P('group', 'member'), may hold values from -8 to 8
- local_lists: int32 [512, 5], P(('group', 'member')), may hold values from -1 to 31, as said below
- remote_lists: int32 [512, 3], P(('group', 'member')), may hold values from -1 to 15, as said below
- send_blocks: int32 [16, 16], P('group'), may hold values from 0 to 31
Outputs:
- attended: bfloat16 [65536, 6144], P(('group', 'member'))
Inputs may be any that keep to these rules, and one draw needn't show every extreme that they name: `local_lists`: row i lists distinct blocks of its slab, numbered 0 to 31 within the slab, then -1 in the remaining entries; the first entry is i mod 32, the row's own block. Some row lists 5 blocks. `remote_lists`: row i lists distinct slabs other than its own slab i // 32, then -1 in the remaining entries; a row may list none. Some row lists 3 slabs.
All inputs are finite; a program needn't handle non-finite values.
Results may differ from a plain program's by a relative error of at most 0.0038.
Values may be sent and summed in bfloat16 or wider, within the bound.
A program may use at most 128 MiB of HBM per device.

v0:
```python
import jax
import jax.numpy as jnp
from jax import lax
from jax.sharding import PartitionSpec as P

HEADS = 48
KV_HEADS = 8
HEAD_DIM = 128


def attend_rows(query_rows, listed, usable):
    block_rows = query_rows.shape[0]
    key_width = KV_HEADS * HEAD_DIM
    repeat = HEADS // KV_HEADS
    query_heads = query_rows.reshape(block_rows, KV_HEADS, repeat, HEAD_DIM)
    keys_all = listed[:, :, :key_width].reshape(
        listed.shape[0], listed.shape[1], KV_HEADS, HEAD_DIM
    )
    values_all = listed[:, :, key_width:].reshape(
        listed.shape[0], listed.shape[1], KV_HEADS, HEAD_DIM
    )
    halves = 2
    head_span = KV_HEADS // halves
    pieces = []
    for part_index in range(halves):
        start_head = part_index * head_span
        query_part = query_heads[:, start_head : start_head + head_span]
        keys_part = keys_all[:, :, start_head : start_head + head_span]
        values_part = values_all[:, :, start_head : start_head + head_span]
        scores = jnp.einsum(
            "qgrd,pkgd->qgrpk", query_part, keys_part, preferred_element_type=jnp.float32
        )
        scores = scores * HEAD_DIM ** (-0.5)
        scores = jnp.where(usable[:, None], scores, -jnp.inf)
        maxima = jnp.max(scores, axis=(3, 4), keepdims=True)
        weights = jnp.exp(scores - maxima)
        totals = jnp.sum(weights, axis=(3, 4))
        rounded = weights.astype(jnp.bfloat16)
        blended = jnp.einsum(
            "qgrpk,pkgd->qgrd", rounded, values_part, preferred_element_type=jnp.float32
        )
        pieces.append(blended / totals[..., None])
    joined = jnp.concatenate(pieces, axis=1)
    return joined.reshape(block_rows, HEADS * HEAD_DIM).astype(jnp.bfloat16)


def shards(queries, keys_values, local_lists, remote_lists, send_blocks):
    targets = send_blocks[0]
    query_count = local_lists.shape[0]
    block_rows = queries.shape[0] // query_count
    outputs = []
    outgoing = jnp.take(keys_values, targets, axis=0)
    arrived = lax.all_to_all(outgoing, "group", split_axis=0, concat_axis=0, tiled=True)
    group_pool = lax.all_gather(keys_values, "member", axis=1, tiled=True)
    cast_pool = lax.all_gather(arrived, "member", axis=1, tiled=True)
    for query_block in range(query_count):
        local_row = local_lists[query_block]
        remote_row = remote_lists[query_block]
        listed = jnp.concatenate(
            [
                jnp.take(group_pool, jnp.maximum(local_row, 0), axis=0),
                jnp.take(cast_pool, jnp.maximum(remote_row, 0), axis=0),
            ],
            axis=0,
        )
        usable = jnp.concatenate([local_row >= 0, remote_row >= 0])
        query_rows = queries[query_block * block_rows : (query_block + 1) * block_rows]
        outputs.append(attend_rows(query_rows, listed, usable))
    return jnp.concatenate(outputs, axis=0)


def solution(mesh):
    placed = (
        P(("group", "member"), None),
        P("group", "member", None),
        P(("group", "member"), None),
        P(("group", "member"), None),
        P("group", None),
    )
    return jax.shard_map(
        shards, mesh=mesh, in_specs=placed, out_specs=P(("group", "member"), None), check_vma=False
    )
```

profile of v0, /device:TPU:1, one launch (start us, length us, event | category | flops | bytes accessed | tf_op | source)
XLA Modules:
  0.0 306.8 jit_solution(815406715089342255)
XLA Ops:
  6.5 0.7 fusion.54
  7.2 0.7 compare_and_fusion.4
  7.9 1.8 gather_fusion
  9.7 0.1 broadcast_select_fusion.4
  9.8 17.9 %all_to_all.5 = bf16[16,8,2048]{2,1,0:T(8,128)(2,1)} all-to-all(bf16[16,8,2048]{2,1,0:T(8,128)(2,1)S(1)} %broadcast_select_fusion.4), channel_id=1, replica_groups=mesh['group'=16,'member'=16] {'group'}, dimensions={0} | all-to-all | bytes 1048576 | tf_op jit(solution)/shard_map/all_to_all | solution.py:53
  27.7 0.0 all-gather.3.cloned.1.call-start
  27.8 0.7 all-gather.3.cloned.1.call-update
  28.5 2.1 fusion.63
  30.6 1.6 copy.82
  32.2 1.6 copy.89
  33.8 0.1 pad_add_fusion
  34.0 50.6 %all-gather.5.cloned.1.call-done = bf16[16,128,2048]{2,1,0:T(8,128)(2,1)} async-done(((bf16[16,8,2048]{2,1,0:T(8,128)(2,1)}), bf16[16,128,2048]{2,1,0:T(8,128)(2,1)}) %all-gather.5.cloned.1.call-update) | async-done | bytes 8388624 | tf_op jit(solution)/shard_map/all_gather | solution.py:55
  84.6 4.0 %gather_fusion.4 = bf16[3,128,2048]{2,1,0:T(8,128)(2,1)S(1)} fusion(bf16[16,128,2048]{2,1,0:T(8,128)(2,1)} %all-gather.5.cloned.1.call-done, s32[1024]{0:T(1024)S(1)} %pad_clamp_fusion), kind=kCustom, calls=%fused_computation.3.clone | custom fusion | bytes 3145740 | tf_op jit(solution)/shard_map/jit(_take)/gather | solution.py:62
  88.6 4.0 %gather_fusion.2 = bf16[3,128,2048]{2,1,0:T(8,128)(2,1)S(1)} fusion(bf16[16,128,2048]{2,1,0:T(8,128)(2,1)} %all-gather.5.cloned.1.call-done, s32[1024]{0:T(1024)S(1)} %pad_clamp_fusion.2), kind=kCustom, calls=%fused_computation.1.clone | custom fusion | bytes 3145740 | tf_op jit(solution)/shard_map/jit(_take)/gather | solution.py:62
  92.7 2.0 broadcast_select_fusion.2
  94.7 85.7 %all-gather.3.cloned.1.call-done = bf16[32,128,2048]{2,1,0:T(8,128)(2,1)} async-done(((bf16[32,8,2048]{2,1,0:T(8,128)(2,1)}), bf16[32,128,2048]{2,1,0:T(8,128)(2,1)}) %all-gather.3.cloned.1.call-update) | async-done | bytes 16777232 | tf_op jit(solution)/shard_map/all_gather | solution.py:54
  180.4 8.1 %gather_fusion.3 = bf16[5,128,2048]{2,1,0:T(8,128)(2,1)} fusion(bf16[32,128,2048]{2,1,0:T(8,128)(2,1)} %all-gather.3.cloned.1.call-done, s32[1024]{0:T(1024)S(1)} %pad_clamp_fusion.1), kind=kCustom, calls=%fused_computation.2.clone | custom fusion | bytes 5242900 | tf_op jit(solution)/shard_map/jit(_take)/gather | solution.py:61
  188.5 8.1 %gather_fusion.1 = bf16[5,128,2048]{2,1,0:T(8,128)(2,1)} fusion(bf16[32,128,2048]{2,1,0:T(8,128)(2,1)} %all-gather.3.cloned.1.call-done, s32[1024]{0:T(1024)S(1)} %pad_clamp_fusion.4), kind=kCustom, calls=%fused_computation.clone | custom fusion | bytes 5242900 | tf_op jit(solution)/shard_map/jit(_take)/gather | solution.py:61
  196.7 3.2 %broadcast_select_fusion = (bf16[5,128,2048]{2,1,0:T(8,128)(2,1)S(1)}, bf16[5,128,2048]{2,1,0:T(8,128)(2,1)S(1)}) fusion(bf16[5,128,2048]{2,1,0:T(8,128)(2,1)} %gather_fusion.3, pred[5]{0:T(512)(128)(4,1)S(1)} %get-tuple-element.37, bf16[5,128,2048]{2,1,0:T(8,128)(2,1)} %gather_fusion.1, pred[5]{0:T(512)(128)(4,1)S(1)} %get-tuple-element.11), kind=kLoop, calls=%fused_computation.42 | loop fusion | flops 2621440 | bytes 10485770 | tf_op jit(solution)/shard_map/jit(_take)/select_n | solution.py:61
  199.9 2.3 fusion.24
  202.1 3.9 %copy.43 = bf16[8,128,1024]{1,2,0:T(8,128)(2,1)} copy(bf16[8,128,1024]{2,1,0:T(8,128)(2,1)} %get-tuple-element.21) | data formatting | bytes 4194304 | tf_op jit(solution)/shard_map/slice | solution.py:19
  206.0 3.1 %fusion.66 = (bf16[8,128,4,128]{1,3,2,0:T(8,128)(2,1)}, bf16[8,128,4,128]{1,3,2,0:T(8,128)(2,1)}) fusion(bf16[8,128,8,128]{1,3,2,0:T(8,128)(2,1)} %bitcast.206), kind=kLoop, calls=%fused_computation.115 | loop fusion | bytes 4194304 | tf_op jit(solution)/shard_map/slice | solution.py:29
  209.1 3.9 %copy.45 = bf16[8,128,1024]{1,2,0:T(8,128)(2,1)} copy(bf16[8,128,1024]{2,1,0:T(8,128)(2,1)} %get-tuple-element.22) | data formatting | bytes 4194304 | tf_op jit(solution)/shard_map/slice | solution.py:16
  213.0 3.1 %fusion.67 = (bf16[8,128,4,128]{1,3,2,0:T(8,128)(2,1)}, bf16[8,128,4,128]{1,3,2,0:T(8,128)(2,1)}) fusion(bf16[8,128,8,128]{1,3,2,0:T(8,128)(2,1)} %bitcast.207), kind=kLoop, calls=%fused_computation.116 | loop fusion | bytes 4194304 | tf_op jit(solution)/shard_map/slice | solution.py:28
  216.2 2.3 copy.88
  218.4 2.3 copy.92
  220.7 3.4 %fusion.25 = (bf16[8,128,1024]{2,1,0:T(8,128)(2,1)}, bf16[8,128,1024]{2,1,0:T(8,128)(2,1)}) fusion(bf16[5,128,2048]{2,1,0:T(8,128)(2,1)S(1)} %get-tuple-element.48, bf16[3,128,2048]{2,1,0:T(8,128)(2,1)} %get-tuple-element.50), kind=kLoop, calls=%fused_computation.45 | loop fusion | flops 8388608 | bytes 8388608 | tf_op jit(solution)/shard_map/concatenate | solution.py:59
  224.2 3.0 copy.32
  227.2 1.5 fusion.64
  228.7 3.0 copy.34
  231.7 1.5 fusion.65
  233.2 2.4 copy.81
  235.6 2.3 copy.85
  237.9 6.3 %bitcast_reduce_fusion.1 = (f32[128,4,6]{0,2,1:T(8,128)S(1)}, f32[4,8,128,128,6]{3,2,4,1,0:T(8,128)}) fusion(pred[8]{0:T(512)(128)(4,1)S(1)} %get-tuple-element.52, bf16[128,8,6,128]{0,3,2,1:T(8,128)(2,1)S(1)} %bitcast.214, bf16[8,128,4,128]{3,1,0,2:T(8,128)(2,1)S(1)} %copy-done.1), kind=kOutput, calls=%fused_computation.9 | convolution fusion | flops 814740480 | bytes 14430720 | tf_op jit(solution)/shard_map/qgrd,pkgd->qgrpk/dot_general | solution.py:30
  244.2 7.5 %fusion.8 = (f32[128,4,6]{0,2,1:T(8,128)S(1)}, f32[128,4,6]{0,2,1:T(8,128)S(1)}, f32[4,8,128,128,6]{3,2,4,1,0:T(8,128)S(1)}) fusion(f32[4,8,128,128,6]{3,2,4,1,0:T(8,128)} %get-tuple-element.42, f32[128,4,6]{0,2,1:T(8,128)S(1)} %get-tuple-element.41, pred[8]{0:T(512)(128)(4,1)S(1)} %get-tuple-element.52, bf16[128,8,6,128]{0,3,2,1:T(8,128)(2,1)S(1)} %bitcast.215, ...), kind=kOutput, calls=%fused_computation.25 | convolution fusion | flops 827320320 | bytes 27042304 | tf_op jit(solution)/shard_map/qgrd,pkgd->qgrpk/dot_general | solution.py:30
  251.7 7.6 %fusion.27 = bf16[128,4,6,128]{0,3,2,1:T(8,128)(2,1)S(1)} fusion(f32[4,8,128,128,6]{3,2,4,1,0:T(8,128)} %get-tuple-element.42, f32[128,4,6]{0,2,1:T(8,128)S(1)} %get-tuple-element.41, pred[8]{0:T(512)(128)(4,1)S(1)} %get-tuple-element.52, bf16[8,128,4,128]{1,3,2,0:T(8,128)(2,1)S(1)} %copy-done.9, f32[128,4,6]{0,2,1:T(8,128)S(1)} %get-tuple-element.9), kind=kOutput, calls=%fused_computation.51 | convolution fusion | flops 818675712 | bytes 14442504 | tf_op jit(solution)/shard_map/qgrpk,pkgd->qgrd/dot_general | solution.py:39
  259.3 2.5 fusion.10
  261.9 3.3 %fusion.26 = bf16[128,4,6,128]{0,3,2,1:T(8,128)(2,1)S(1)} fusion(f32[4,8,128,128,6]{3,2,4,1,0:T(8,128)S(1)} %get-tuple-element.43, f32[128,4,6]{0,2,1:T(8,128)S(1)} %get-tuple-element.10, pred[8]{0:T(512)(128)(4,1)S(1)} %get-tuple-element.52, bf16[8,128,4,128]{1,3,2,0:T(8,128)(2,1)S(1)} %copy-done.7, f32[128,4,6]{0,2,1:T(8,128)S(1)} %fusion.10), kind=kOutput, calls=%fused_computation.49 | convolution fusion | flops 818675712 | bytes 14442504 | tf_op jit(solution)/shard_map/qgrpk,pkgd->qgrd/dot_general | solution.py:39
  265.1 0.1 pad_maximum_fusion.4
  265.3 0.7 copy.55
  266.0 7.9 %bitcast_reduce_fusion.3 = (f32[128,4,6]{0,2,1:T(8,128)S(1)}, f32[4,8,128,128,6]{3,2,4,1,0:T(8,128)}) fusion(pred[8]{0:T(512)(128)(4,1)S(1)} %get-tuple-element.51, bf16[128,8,6,128]{0,3,2,1:T(8,128)(2,1)} %bitcast.212, bf16[8,128,4,128]{3,1,0,2:T(8,128)(2,1)} %copy.81), kind=kOutput, calls=%fused_computation.15 | convolution fusion | flops 814740480 | bytes 14430216 | tf_op jit(solution)/shard_map/qgrd,pkgd->qgrpk/dot_general | solution.py:30
  273.9 7.5 %fusion.4 = (f32[128,4,6]{0,2,1:T(8,128)S(1)}, f32[128,4,6]{0,2,1:T(8,128)S(1)}, f32[4,8,128,128,6]{3,2,4,1,0:T(8,128)S(1)}) fusion(f32[4,8,128,128,6]{3,2,4,1,0:T(8,128)} %get-tuple-element.45, f32[128,4,6]{0,2,1:T(8,128)S(1)} %get-tuple-element.44, pred[8]{0:T(512)(128)(4,1)S(1)} %get-tuple-element.51, bf16[128,8,6,128]{0,3,2,1:T(8,128)(2,1)S(1)} %bitcast.213, ...), kind=kOutput, calls=%fused_computation.21 | convolution fusion | flops 827320320 | bytes 27042304 | tf_op jit(solution)/shard_map/qgrd,pkgd->qgrpk/dot_general | solution.py:30
  281.4 7.6 %fusion.29 = bf16[128,4,6,128]{0,3,2,1:T(8,128)(2,1)S(1)} fusion(f32[4,8,128,128,6]{3,2,4,1,0:T(8,128)} %get-tuple-element.45, f32[128,4,6]{0,2,1:T(8,128)S(1)} %get-tuple-element.44, pred[8]{0:T(512)(128)(4,1)S(1)} %get-tuple-element.51, bf16[8,128,4,128]{1,3,2,0:T(8,128)(2,1)S(1)} %copy-done.8, f32[128,4,6]{0,2,1:T(8,128)S(1)} %get-tuple-element.6), kind=kOutput, calls=%fused_computation.55 | convolution fusion | flops 818675712 | bytes 14442504 | tf_op jit(solution)/shard_map/qgrpk,pkgd->qgrd/dot_general | solution.py:39
  289.1 2.5 fusion.6
  291.6 3.3 %fusion.28 = bf16[128,4,6,128]{0,3,2,1:T(8,128)(2,1)S(1)} fusion(f32[4,8,128,128,6]{3,2,4,1,0:T(8,128)S(1)} %get-tuple-element.46, f32[128,4,6]{0,2,1:T(8,128)S(1)} %get-tuple-element.8, pred[8]{0:T(512)(128)(4,1)S(1)} %get-tuple-element.51, bf16[8,128,4,128]{1,3,2,0:T(8,128)(2,1)S(1)} %copy-done.6, f32[128,4,6]{0,2,1:T(8,128)S(1)} %fusion.6), kind=kOutput, calls=%fused_computation.53 | convolution fusion | flops 818675712 | bytes 14442504 | tf_op jit(solution)/shard_map/qgrpk,pkgd->qgrd/dot_general | solution.py:39
  294.9 0.1 pad_maximum_fusion.3
  295.0 1.6 copy.54
  296.6 3.3 %pad_maximum_fusion = bf16[256,6144]{1,0:T(8,128)(2,1)} fusion(bf16[128,6144]{1,0:T(8,128)(2,1)S(1)} %copy.55, bf16[128,6144]{1,0:T(8,128)(2,1)} %copy.54), kind=kLoop, calls=%fused_computation.41 | loop fusion | flops 6291456 | bytes 6291456 | tf_op jit(solution)/shard_map/concatenate | solution.py:69
  (35 shorter events, 0.1 us)
Async XLA Ops:
  6.5 78.1 %all-gather.5.cloned.1.call-start = ((), (), s32[]{:S(2)}) async-start(), calls=%async_computation.2 | async-start | bytes 8912896 | tf_op jit(solution)/shard_map/all_gather | solution.py:55
  27.7 152.7 %all-gather.3.cloned.1.call-start = ((), (), s32[]{:S(2)}) async-start(), calls=%async_computation.1 | async-start | bytes 17825792 | tf_op jit(solution)/shard_map/all_gather | solution.py:54
  30.6 3.2 %copy-start.11 = (s32[2,5]{1,0:T(2,128)S(1)}, s32[2,5]{1,0:T(2,128)}, u32[]{:S(2)}) copy-start(s32[2,5]{1,0:T(2,128)} %param.11) | copy-start | bytes 124
  30.6 3.2 %copy-start.10 = (s32[2,3]{1,0:T(2,128)S(1)}, s32[2,3]{1,0:T(2,128)}, u32[]{:S(2)}) copy-start(s32[2,3]{1,0:T(2,128)} %param.12) | copy-start | bytes 76
  196.7 3.2 %copy-start = (bf16[3,128,2048]{2,1,0:T(8,128)(2,1)S(1)}, bf16[3,128,2048]{2,1,0:T(8,128)(2,1)}, u32[]{:S(2)}) copy-start(bf16[3,128,2048]{2,1,0:T(8,128)(2,1)} %get-tuple-element.49) | copy-start | bytes 4718596
  231.7 6.2 %copy-start.1 = (bf16[8,128,4,128]{3,1,0,2:T(8,128)(2,1)S(1)}, bf16[8,128,4,128]{3,1,0,2:T(8,128)(2,1)}, u32[]{:S(2)}) copy-start(bf16[8,128,4,128]{3,1,0,2:T(8,128)(2,1)} %copy.88) | copy-start | bytes 3145732
  233.2 4.7 %copy-start.3 = (bf16[128,6144]{0,1:T(8,128)(2,1)S(1)}, bf16[128,6144]{0,1:T(8,128)(2,1)}, u32[]{:S(2)}) copy-start(bf16[128,6144]{0,1:T(8,128)(2,1)} %copy.89) | copy-start | bytes 4718596
  237.9 6.3 %copy-start.5 = (bf16[8,128,4,128]{3,1,0,2:T(8,128)(2,1)S(1)}, bf16[8,128,4,128]{3,1,0,2:T(8,128)(2,1)}, u32[]{:S(2)}) copy-start(bf16[8,128,4,128]{3,1,0,2:T(8,128)(2,1)} %copy.92) | copy-start | bytes 3145732
  244.2 7.5 %copy-start.9 = (bf16[8,128,4,128]{1,3,2,0:T(8,128)(2,1)S(1)}, bf16[8,128,4,128]{1,3,2,0:T(8,128)(2,1)}, u32[]{:S(2)}) copy-start(bf16[8,128,4,128]{1,3,2,0:T(8,128)(2,1)} %get-tuple-element.29) | copy-start | bytes 3145732
  259.3 2.5 copy-start.7
  266.0 7.9 %copy-start.2 = (bf16[128,6144]{0,1:T(8,128)(2,1)S(1)}, bf16[128,6144]{0,1:T(8,128)(2,1)}, u32[]{:S(2)}) copy-start(bf16[128,6144]{0,1:T(8,128)(2,1)} %copy.82) | copy-start | bytes 4718596
  266.0 7.9 %copy-start.4 = (bf16[8,128,4,128]{3,1,0,2:T(8,128)(2,1)S(1)}, bf16[8,128,4,128]{3,1,0,2:T(8,128)(2,1)}, u32[]{:S(2)}) copy-start(bf16[8,128,4,128]{3,1,0,2:T(8,128)(2,1)} %copy.85) | copy-start | bytes 3145732
  273.9 7.5 %copy-start.8 = (bf16[8,128,4,128]{1,3,2,0:T(8,128)(2,1)S(1)}, bf16[8,128,4,128]{1,3,2,0:T(8,128)(2,1)}, u32[]{:S(2)}) copy-start(bf16[8,128,4,128]{1,3,2,0:T(8,128)(2,1)} %get-tuple-element.25) | copy-start | bytes 3145732
  289.1 2.5 copy-start.6
Sparse Core Ops, SparseCore 0:
  27.8 56.7 all-gather.4
  86.5 93.9 all-gather.2
where the time goes:
time: 308 us; the launch traced here: 307 us
  waiting for transfers between devices  137 us (44%)
  local copies, waits for them, and re-layouts  66 us (21%)
  matrix products  51 us (17%)
  other arithmetic  21.1 us (7%)
  blocking collectives  17.9 us (6%)
  between operations  13.7 us (4%)
    all_gather x1, waiting for transfers between devices, shards(): group_pool = lax.all_gather(keys_values, 'member', axis=1, tiled=True)  85.7 us
    all_gather x1, waiting for transfers between devices, shards(): cast_pool = lax.all_gather(arrived, 'member', axis=1, tiled=True)  50.6 us
    dot_general x4, matrix products, attend_rows(): jnp.einsum('qgrd,pkgd->qgrpk', query_part, keys_part, preferred_element_t...  29.2 us
    dot_general x4, matrix products, attend_rows(): jnp.einsum('qgrpk,pkgd->qgrd', rounded, values_part, preferred_element_ty...  21.8 us
    all_to_all x1, blocking collectives, shards(): lax.all_to_all(outgoing, 'group', split_axis=0, concat_axis=0, tiled=True)  17.9 us
    gather x2, local copies, waits for them, and re-layouts, shards(): jnp.take(group_pool, jnp.maximum(local_row, 0), axis=0)  16.3 us
    unnamed x30, local copies, waits for them, and re-layouts  12.5 us
    gather x2, local copies, waits for them, and re-layouts, shards(): jnp.take(cast_pool, jnp.maximum(remote_row, 0), axis=0)  8.06 us
  transfers between devices with their start and end apart: 2, of which 2 were waited for; matrix products, arithmetic and copies ran while one was open for 5% of the time, Pallas kernels for 0%

commit v1 on v0

--- a/solution.py
+++ b/solution.py
@@ -51,8 +51,13 @@
     outputs = []
     outgoing = jnp.take(keys_values, targets, axis=0)
     arrived = lax.all_to_all(outgoing, "group", split_axis=0, concat_axis=0, tiled=True)
-    group_pool = lax.all_gather(keys_values, "member", axis=1, tiled=True)
-    cast_pool = lax.all_gather(arrived, "member", axis=1, tiled=True)
+    group_pool, cast_pool = jnp.split(
+        jax.lax.all_gather(
+            jnp.concatenate([keys_values, arrived], axis=0), "member", tiled=True, axis=1
+        ),
+        [keys_values.shape[0]],
+        axis=0,
+    )
     for query_block in range(query_count):
         local_row = local_lists[query_block]
         remote_row = remote_lists[query_block]

time: 308 us -> 328 us (1.065)
  local copies, waits for them, and re-layouts: 66 us -> 92.2 us
  waiting for transfers between devices: 137 us -> 130 us
    split x0 -> x2, local copies, waits for them, and re-layouts: none -> 22.4 us  [shards(): jnp.split(jax.lax.all_gather(jnp.concatenate([keys_values, arrived], axis...]
    all_gather x2 -> x1, waiting for transfers between devices: 136 us -> 130 us  [shards(): jax.lax.all_gather(jnp.concatenate([keys_values, arrived], axis=0), 'memb...]
  transfers between devices with their start and end apart: 2 -> 1, of which waited for: 2 -> 1; matrix products, arithmetic and copies ran while one was open for 5% -> 2% of each run, Pallas kernels for 0% -> 0%
where the time goes in v1:
time: 328 us; the launch traced here: 327 us
  waiting for transfers between devices  130 us (40%)
  local copies, waits for them, and re-layouts  92.2 us (28%)
  matrix products  48.9 us (15%)
  other arithmetic  24.3 us (7%)
  blocking collectives  17.8 us (5%)
  between operations  13.7 us (4%)
    all_gather x1, waiting for transfers between devices, shards(): jax.lax.all_gather(jnp.concatenate([keys_values, arrived], axis=0), 'memb...  130 us
    dot_general x4, matrix products, attend_rows(): jnp.einsum('qgrd,pkgd->qgrpk', query_part, keys_part, preferred_element_t...  27.2 us
    split x2, local copies, waits for them, and re-layouts, shards(): jnp.split(jax.lax.all_gather(jnp.concatenate([keys_values, arrived], axis...  22.4 us
    dot_general x4, matrix products, attend_rows(): jnp.einsum('qgrpk,pkgd->qgrd', rounded, values_part, preferred_element_ty...  21.7 us
    all_to_all x1, blocking collectives, shards(): lax.all_to_all(outgoing, 'group', split_axis=0, concat_axis=0, tiled=True)  17.8 us
    gather x2, local copies, waits for them, and re-layouts, shards(): jnp.take(group_pool, jnp.maximum(local_row, 0), axis=0)  16.3 us
    unnamed x30, local copies, waits for them, and re-layouts  12.6 us
    gather x2, local copies, waits for them, and re-layouts, shards(): jnp.take(cast_pool, jnp.maximum(remote_row, 0), axis=0)  10.4 us
  transfers between devices with their start and end apart: 1, of which 1 were waited for; matrix products, arithmetic and copies ran while one was open for 2% of the time, Pallas kernels for 0%

profile of v1, /device:TPU:1, one launch (start us, length us, event | category | flops | bytes accessed | tf_op | source)
XLA Modules:
  0.0 327.2 jit_solution(9303991316539019739)
XLA Ops:
  6.5 0.7 fusion.54
  7.2 0.7 compare_and_fusion.4
  7.9 1.8 gather_fusion
  9.8 17.8 %all_to_all.5 = bf16[16,8,2048]{2,1,0:T(8,128)(2,1)S(1)} all-to-all(bf16[16,8,2048]{2,1,0:T(8,128)(2,1)S(1)} %broadcast_select_fusion.4), channel_id=1, replica_groups=mesh['group'=16,'member'=16] {'group'}, dimensions={0} | all-to-all | bytes 1048576 | tf_op jit(solution)/shard_map/all_to_all | solution.py:53
  27.6 2.5 pad_maximum_fusion.3
  30.1 2.1 fusion.63
  32.2 1.6 copy.82
  33.8 1.6 copy.89
  35.6 130.4 %all-gather.2.cloned.1.call-done = bf16[48,128,2048]{2,1,0:T(8,128)(2,1)} async-done(((bf16[48,8,2048]{2,1,0:T(8,128)(2,1)}), bf16[48,128,2048]{2,1,0:T(8,128)(2,1)}) %all-gather.2.cloned.1.call-update) | async-done | bytes 25165840 | tf_op jit(solution)/shard_map/all_gather | solution.py:55
  166.0 14.1 %split.8 = bf16[32,128,2048]{2,1,0:T(8,128)(2,1)} slice(bf16[48,128,2048]{2,1,0:T(8,128)(2,1)} %all-gather.2.cloned.1.call-done), slice={[0:32], [0:128], [0:2048]} | slice | bytes 33554432 | tf_op jit(solution)/shard_map/split | solution.py:54
  180.1 8.2 %gather_fusion.1 = bf16[5,128,2048]{2,1,0:T(8,128)(2,1)} fusion(bf16[32,128,2048]{2,1,0:T(8,128)(2,1)} %split.8, s32[1024]{0:T(1024)S(1)} %pad_clamp_fusion.3), kind=kCustom, calls=%fused_computation.clone | custom fusion | bytes 5242900 | tf_op jit(solution)/shard_map/jit(_take)/gather | solution.py:66
  188.3 8.1 %gather_fusion.3 = bf16[5,128,2048]{2,1,0:T(8,128)(2,1)} fusion(bf16[32,128,2048]{2,1,0:T(8,128)(2,1)} %split.8, s32[1024]{0:T(1024)S(1)} %pad_clamp_fusion.1), kind=kCustom, calls=%fused_computation.2.clone | custom fusion | bytes 5242900 | tf_op jit(solution)/shard_map/jit(_take)/gather | solution.py:66
  196.4 8.3 %split.9 = bf16[16,128,2048]{2,1,0:T(8,128)(2,1)} slice(bf16[48,128,2048]{2,1,0:T(8,128)(2,1)} %all-gather.2.cloned.1.call-done), slice={[32:48], [0:128], [0:2048]} | slice | bytes 16777216 | tf_op jit(solution)/shard_map/split | solution.py:54
  204.7 5.2 %gather_fusion.2 = bf16[3,128,2048]{2,1,0:T(8,128)(2,1)} fusion(bf16[16,128,2048]{2,1,0:T(8,128)(2,1)} %split.9, s32[1024]{0:T(1024)S(1)} %pad_clamp_fusion.2), kind=kCustom, calls=%fused_computation.1.clone | custom fusion | bytes 3145740 | tf_op jit(solution)/shard_map/jit(_take)/gather | solution.py:67
  209.9 5.2 %gather_fusion.4 = bf16[3,128,2048]{2,1,0:T(8,128)(2,1)} fusion(bf16[16,128,2048]{2,1,0:T(8,128)(2,1)} %split.9, s32[1024]{0:T(1024)S(1)} %pad_clamp_fusion), kind=kCustom, calls=%fused_computation.3.clone | custom fusion | bytes 3145740 | tf_op jit(solution)/shard_map/jit(_take)/gather | solution.py:67
  215.1 3.2 broadcast_select_fusion
  218.3 0.2 copy-done.2
  218.5 1.5 broadcast_select_fusion.2
  220.1 2.3 fusion.25
  222.3 3.9 %copy.34 = bf16[8,128,1024]{1,2,0:T(8,128)(2,1)} copy(bf16[8,128,1024]{2,1,0:T(8,128)(2,1)} %get-tuple-element.20) | data formatting | bytes 4194304 | tf_op jit(solution)/shard_map/slice | solution.py:16
  226.2 3.1 fusion.65
  229.3 2.3 copy.81
  231.6 2.3 copy.85
  233.9 3.9 %copy.32 = bf16[8,128,1024]{1,2,0:T(8,128)(2,1)} copy(bf16[8,128,1024]{2,1,0:T(8,128)(2,1)} %get-tuple-element.19) | data formatting | bytes 4194304 | tf_op jit(solution)/shard_map/slice | solution.py:19
  237.8 2.9 fusion.64
  240.7 6.3 %bitcast_reduce_fusion.3 = (f32[128,4,6]{0,2,1:T(8,128)S(1)}, f32[4,8,128,128,6]{3,2,4,1,0:T(8,128)}) fusion(pred[8]{0:T(512)(128)(4,1)S(1)} %get-tuple-element.51, bf16[128,8,6,128]{0,3,2,1:T(8,128)(2,1)S(1)} %bitcast.214, bf16[8,128,4,128]{3,1,0,2:T(8,128)(2,1)S(1)} %copy-done.3), kind=kOutput, calls=%fused_computation.15 | convolution fusion | flops 814740480 | bytes 14430720 | tf_op jit(solution)/shard_map/qgrd,pkgd->qgrpk/dot_general | solution.py:30
  247.0 7.4 %fusion.4 = (f32[128,4,6]{0,2,1:T(8,128)S(1)}, f32[128,4,6]{0,2,1:T(8,128)S(1)}, f32[4,8,128,128,6]{3,2,4,1,0:T(8,128)S(1)}) fusion(f32[4,8,128,128,6]{3,2,4,1,0:T(8,128)} %get-tuple-element.45, f32[128,4,6]{0,2,1:T(8,128)S(1)} %get-tuple-element.44, pred[8]{0:T(512)(128)(4,1)S(1)} %get-tuple-element.51, bf16[128,8,6,128]{0,3,2,1:T(8,128)(2,1)S(1)} %bitcast.215, ...), kind=kOutput, calls=%fused_computation.21 | convolution fusion | flops 827320320 | bytes 27042304 | tf_op jit(solution)/shard_map/qgrd,pkgd->qgrpk/dot_general | solution.py:30
  254.4 7.6 %fusion.29 = bf16[128,4,6,128]{0,3,2,1:T(8,128)(2,1)S(1)} fusion(f32[4,8,128,128,6]{3,2,4,1,0:T(8,128)} %get-tuple-element.45, f32[128,4,6]{0,2,1:T(8,128)S(1)} %get-tuple-element.44, pred[8]{0:T(512)(128)(4,1)S(1)} %get-tuple-element.51, bf16[8,128,4,128]{1,3,2,0:T(8,128)(2,1)S(1)} %get-tuple-element.25, f32[128,4,6]{0,2,1:T(8,128)S(1)} %get-tuple-element.6), kind=kOutput, calls=%fused_computation.55 | convolution fusion | flops 818675712 | bytes 14442504 | tf_op jit(solution)/shard_map/qgrpk,pkgd->qgrd/dot_general | solution.py:39
  262.0 2.5 fusion.6
  264.6 3.3 fusion.28
  267.9 1.3 pad_maximum_fusion.4
  269.1 2.6 copy.54
  271.7 3.4 %fusion.24 = (bf16[8,128,1024]{2,1,0:T(8,128)(2,1)}, bf16[8,128,1024]{2,1,0:T(8,128)(2,1)}) fusion(bf16[5,128,2048]{2,1,0:T(8,128)(2,1)S(1)} %get-tuple-element.47, bf16[3,128,2048]{2,1,0:T(8,128)(2,1)} %get-tuple-element.49), kind=kLoop, calls=%fused_computation.44 | loop fusion | flops 8388608 | bytes 8388608 | tf_op jit(solution)/shard_map/concatenate | solution.py:64
  275.1 3.0 copy.45
  278.2 1.5 fusion.67
  279.6 1.6 copy.88
  281.2 2.3 copy.92
  283.5 3.0 copy.43
  286.6 1.1 fusion.66
  287.7 0.7 copy-done.4
  288.4 6.3 %bitcast_reduce_fusion.1 = (f32[128,4,6]{0,2,1:T(8,128)S(1)}, f32[4,8,128,128,6]{3,2,4,1,0:T(8,128)}) fusion(pred[8]{0:T(512)(128)(4,1)S(1)} %get-tuple-element.52, bf16[128,8,6,128]{0,3,2,1:T(8,128)(2,1)S(1)} %bitcast.212, bf16[8,128,4,128]{3,1,0,2:T(8,128)(2,1)S(1)} %copy.88), kind=kOutput, calls=%fused_computation.9 | convolution fusion | flops 814740480 | bytes 14430720 | tf_op jit(solution)/shard_map/qgrd,pkgd->qgrpk/dot_general | solution.py:30
  294.7 7.2 %fusion.8 = (f32[128,4,6]{0,2,1:T(8,128)S(1)}, f32[128,4,6]{0,2,1:T(8,128)S(1)}, f32[4,8,128,128,6]{3,2,4,1,0:T(8,128)S(1)}) fusion(f32[4,8,128,128,6]{3,2,4,1,0:T(8,128)} %get-tuple-element.42, f32[128,4,6]{0,2,1:T(8,128)S(1)} %get-tuple-element.41, pred[8]{0:T(512)(128)(4,1)S(1)} %get-tuple-element.52, bf16[128,8,6,128]{0,3,2,1:T(8,128)(2,1)S(1)} %bitcast.213, ...), kind=kOutput, calls=%fused_computation.25 | convolution fusion | flops 827320320 | bytes 27042304 | tf_op jit(solution)/shard_map/qgrd,pkgd->qgrpk/dot_general | solution.py:30
  301.9 7.6 %fusion.27 = bf16[128,4,6,128]{0,3,2,1:T(8,128)(2,1)S(1)} fusion(f32[4,8,128,128,6]{3,2,4,1,0:T(8,128)} %get-tuple-element.42, f32[128,4,6]{0,2,1:T(8,128)S(1)} %get-tuple-element.41, pred[8]{0:T(512)(128)(4,1)S(1)} %get-tuple-element.52, bf16[8,128,4,128]{1,3,2,0:T(8,128)(2,1)S(1)} %get-tuple-element.29, f32[128,4,6]{0,2,1:T(8,128)S(1)} %get-tuple-element.9), kind=kOutput, calls=%fused_computation.51 | convolution fusion | flops 818675712 | bytes 14442504 | tf_op jit(solution)/shard_map/qgrpk,pkgd->qgrd/dot_general | solution.py:39
  309.5 2.5 fusion.10
  312.0 3.3 fusion.26
  315.3 0.1 pad_maximum_fusion.5
  315.4 1.6 copy.55
  317.0 3.4 %pad_maximum_fusion = bf16[256,6144]{1,0:T(8,128)(2,1)} fusion(bf16[128,6144]{1,0:T(8,128)(2,1)} %copy.55, bf16[128,6144]{1,0:T(8,128)(2,1)S(1)} %copy-done), kind=kLoop, calls=%fused_computation.41 | loop fusion | flops 6291456 | bytes 6291456 | tf_op jit(solution)/shard_map/concatenate | solution.py:74
  (35 shorter events, 0.3 us)
Async XLA Ops:
  6.5 159.5 %all-gather.2.cloned.1.call-start = ((), (), s32[]{:S(2)}) async-start(), calls=%async_computation.1 | async-start | bytes 26738688 | tf_op jit(solution)/shard_map/all_gather | solution.py:55
  32.2 3.2 copy-start.10
  32.2 3.2 copy-start.11
  215.1 3.2 copy-start.1
  215.1 3.4 %copy-start.2 = (bf16[3,128,2048]{2,1,0:T(8,128)(2,1)S(1)}, bf16[3,128,2048]{2,1,0:T(8,128)(2,1)}, u32[]{:S(2)}) copy-start(bf16[3,128,2048]{2,1,0:T(8,128)(2,1)} %gather_fusion.4) | copy-start | bytes 4718596
  237.8 2.9 copy-start.3
  237.8 2.9 copy-start.5
  240.7 6.3 %copy-start.7 = (bf16[8,128,4,128]{3,1,0,2:T(8,128)(2,1)S(1)}, bf16[8,128,4,128]{3,1,0,2:T(8,128)(2,1)}, u32[]{:S(2)}) copy-start(bf16[8,128,4,128]{3,1,0,2:T(8,128)(2,1)} %copy.85) | copy-start | bytes 3145732
  262.0 2.6 copy-start.9
  286.6 1.8 copy-start.4
  288.4 6.3 %copy-start.6 = (bf16[8,128,4,128]{3,1,0,2:T(8,128)(2,1)S(1)}, bf16[8,128,4,128]{3,1,0,2:T(8,128)(2,1)}, u32[]{:S(2)}) copy-start(bf16[8,128,4,128]{3,1,0,2:T(8,128)(2,1)} %copy.92) | copy-start | bytes 3145732
  309.5 2.5 copy-start.8
  315.3 1.8 copy-start
Sparse Core Ops, SparseCore 0:
  30.2 135.7 all-gather.1
